TPU v7x, 256 devices: a whole 4x4x8 slice. The times are simulated.
256 devices in a mesh: dp: 2 (over core), ctx: 32 (over y, z), grp: 4 (over x).
Axes of the slice: x: 4, y: 4, z: 8, core: 2. Of those that a mesh axis runs over, the one named last changes fastest.
Arguments:
- projected: bfloat16 [4, 8192, 3, 4096], P('dp', 'ctx', None, 'grp'), may hold values from -6 to 6
- short_w: float32 [3, 3, 4096], P(None, None, 'grp'), may hold values from -2.5 to 2.5
- medium_h: bfloat16 [256, 128], P('grp'), may hold values from -3 to 3
- out_w: bfloat16 [4096, 4096], P('ctx', 'grp'), may hold values from -0.09375 to 0.09375
- grad_out: bfloat16 [4, 8192, 4096], P('dp', 'ctx', 'grp'), may hold values from -6 to 6
Outputs:
- block_out: bfloat16 [4, 8192, 4096], P('dp', 'ctx', 'grp')
- grad_projected: bfloat16 [4, 8192, 3, 4096], P('dp', 'ctx', None, 'grp')
- filter_grad: float32 [256, 128], P('grp')
- short_grad: float32 [3, 3, 4096], P(None, None, 'grp')
All inputs are finite; a program needn't handle non-finite values.
Results may differ from a plain program's by a relative error of at most 0.0064.
Values may be sent and summed in bfloat16 or wider, within the bound.
A program may use at most 128 MiB of HBM per device.

v0:
```python
import math
import jax
import jax.numpy as jnp
from jax import lax
from jax.sharding import PartitionSpec as P


def from_behind(block, axis, distance):
    devices = range(lax.axis_size(axis))
    route = [(i - distance, i) for i in devices if i - distance in devices]
    return lax.ppermute(block, axis, route)


def windows(padded, block_rows, reach):
    seqs_here = padded.shape[0]
    block_count = (padded.shape[1] - reach) // block_rows
    extended = jnp.pad(padded, ((0, 0), (0, block_rows - reach), (0, 0), (0, 0)))
    leading = extended[:, : block_count * block_rows].reshape(
        seqs_here, block_count, block_rows, padded.shape[2], padded.shape[3]
    )
    second = extended[:, block_rows:].reshape(
        seqs_here, block_count, block_rows, padded.shape[2], padded.shape[3]
    )[:, :, :reach]
    return jnp.concatenate([leading, second], axis=2)


def banded(filters, block_rows):
    groups_here = filters.shape[0]
    tap_count = filters.shape[1]
    line_width = block_rows + tap_count
    padded_line = jnp.concatenate(
        [filters, jnp.zeros((groups_here, block_rows), filters.dtype)], axis=1
    )
    tiled = jnp.broadcast_to(
        padded_line[:, None, :], (groups_here, block_rows, line_width)
    ).reshape(groups_here, block_rows * line_width)
    return tiled[:, : block_rows * (line_width - 1)].reshape(
        groups_here, block_rows, line_width - 1
    )


def band_conv(turned, matrix, block_rows):
    reach = matrix.shape[2] - block_rows
    windowed = windows(turned, block_rows, reach)
    result = jnp.einsum("gtj,sbjcg->sbtcg", matrix, windowed, preferred_element_type=jnp.float32)
    result = jnp.swapaxes(result, 3, 4)
    return result.reshape(
        turned.shape[0], turned.shape[1] - reach, turned.shape[2] * turned.shape[3]
    )


def lag_sums(grad_blocks, windowed, tap_count):
    products = jnp.einsum(
        "sbtcg,sbjcg->gtj", grad_blocks, windowed, preferred_element_type=jnp.float32
    )
    groups_here = products.shape[0]
    block_rows = products.shape[1]
    line_width = products.shape[2]
    flat_rows = jnp.pad(
        products.reshape(groups_here, block_rows * line_width), ((0, 0), (0, block_rows))
    )
    skewed = flat_rows.reshape(groups_here, block_rows, line_width + 1)[:, :, :tap_count]
    return jnp.sum(skewed, axis=1)[:, ::-1]


def featurize(padded, weights):
    short_reach = weights.shape[1] - 1
    row_count = padded.shape[1] - short_reach
    total = None
    for offset in range(weights.shape[1]):
        start = short_reach - offset
        term = weights[:, offset, :] * padded[:, start : start + row_count]
        total = term if total is None else total + term
    return total


def adjoint(padded, weights):
    short_reach = weights.shape[1] - 1
    row_count = padded.shape[1] - short_reach
    total = None
    for offset in range(weights.shape[1]):
        term = weights[:, offset, :] * padded[:, offset : offset + row_count]
        total = term if total is None else total + term
    return total


def short_sums(feature_grad, padded, short_taps):
    row_count = feature_grad.shape[1]
    short_reach = short_taps - 1
    terms = []
    for offset in range(short_taps):
        start = short_reach - offset
        terms.append(jnp.sum(feature_grad * padded[:, start : start + row_count], axis=(0, 1)))
    return jnp.stack(terms, axis=1)


def shards(projected, short_w, medium_h, out_w, grad_out):
    seq_local = projected.shape[0]
    row_count = projected.shape[1]
    chan_local = projected.shape[3]
    tap_count = medium_h.shape[1]
    reach = tap_count - 1
    short_taps = short_w.shape[1]
    short_reach = short_taps - 1
    group_local = medium_h.shape[0]
    group_size = chan_local // group_local
    block_rows = math.gcd(row_count, 128)
    front_rows = from_behind(projected[:, row_count - short_reach :], "ctx", 1)
    padded_input = jnp.concatenate([front_rows, projected], axis=1)
    features = featurize(padded_input.astype(jnp.float32), short_w)
    product = (features[:, :, 1] * features[:, :, 2]).astype(jnp.bfloat16)
    product_front = from_behind(product[:, row_count - reach :], "ctx", 1)
    product_pad = jnp.concatenate([product_front, product], axis=1)
    query = features[:, :, 0]
    keys = features[:, :, 1]
    values = features[:, :, 2]
    product_turned = jnp.swapaxes(
        product_pad.reshape(seq_local, row_count + reach, group_local, group_size), 2, 3
    )
    mixed = band_conv(product_turned, banded(medium_h[:, ::-1], block_rows), block_rows)
    gated = (query * mixed).astype(jnp.bfloat16)
    whole_gated = lax.all_gather(gated, "grp", axis=2, tiled=True)
    flat_gated = whole_gated.reshape(seq_local * row_count, whole_gated.shape[2])
    flat_cotangent = grad_out.reshape(seq_local * row_count, chan_local)
    projected_out = jnp.dot(
        flat_gated,
        lax.all_gather(out_w, "ctx", axis=0, tiled=True),
        preferred_element_type=jnp.float32,
    )
    block_out = projected_out.astype(jnp.bfloat16).reshape(seq_local, row_count, chan_local)
    input_part = lax.dot_general(
        flat_cotangent,
        lax.all_gather(out_w, "ctx", axis=0, tiled=True),
        (((1,), (1,)), ((), ())),
        preferred_element_type=jnp.float32,
    )
    summed = lax.psum_scatter(input_part, "grp", scatter_dimension=1, tiled=True)
    gated_grad = (
        lax.optimization_barrier(summed.astype(jnp.bfloat16))
        .astype(jnp.float32)
        .reshape(seq_local, row_count, chan_local)
    )
    query_grad = gated_grad * mixed
    mix_grad = (gated_grad * query).astype(jnp.bfloat16)
    mix_back = from_behind(mix_grad[:, :reach], "ctx", -1)
    mix_turned = jnp.swapaxes(
        jnp.concatenate([mix_grad, mix_back], axis=1).reshape(
            seq_local, row_count + reach, group_local, group_size
        ),
        2,
        3,
    )
    product_grad = band_conv(mix_turned, banded(medium_h, block_rows), block_rows)
    grad_blocks = jnp.swapaxes(
        mix_grad.reshape(seq_local, row_count // block_rows, block_rows, group_local, group_size),
        3,
        4,
    )
    filter_part = lag_sums(grad_blocks, windows(product_turned, block_rows, reach), tap_count)
    feature_grad = jnp.stack(
        [query_grad, product_grad * values, product_grad * keys], axis=2
    ).astype(jnp.bfloat16)
    grad_back = from_behind(feature_grad[:, :short_reach], "ctx", -1)
    grad_pad = jnp.concatenate([feature_grad, grad_back], axis=1).astype(jnp.float32)
    grad_projected = adjoint(grad_pad, short_w).astype(jnp.bfloat16)
    short_part = short_sums(
        feature_grad.astype(jnp.float32), padded_input.astype(jnp.float32), short_taps
    )
    filter_total, short_total = lax.psum((filter_part, short_part), ("dp", "ctx"))
    seq_total = seq_local * lax.axis_size("dp")
    length_total = row_count * lax.axis_size("ctx")
    filter_grad = filter_total / math.sqrt(seq_total * length_total * group_size)
    short_grad = short_total / math.sqrt(seq_total * length_total)
    return (block_out, grad_projected, filter_grad, short_grad)


def solution(mesh):
    in_specs = (
        P("dp", "ctx", None, "grp"),
        P(None, None, "grp"),
        P("grp", None),
        P("ctx", "grp"),
        P("dp", "ctx", "grp"),
    )
    out_specs = (
        P("dp", "ctx", "grp"),
        P("dp", "ctx", None, "grp"),
        P("grp", None),
        P(None, None, "grp"),
    )
    return jax.shard_map(shards, mesh=mesh, in_specs=in_specs, out_specs=out_specs, check_vma=False)
```

profile of v0, /device:TPU:1, one launch (start us, length us, event | category | flops | bytes accessed | tf_op | source)
XLA Modules:
  0.0 600.7 jit_solution(14814459723128327061)
XLA Ops:
  8.0 103.6 %all-gather.5.cloned.1.call-done = bf16[4096,1024]{1,0:T(8,128)(2,1)} async-done(((bf16[128,1024]{1,0:T(8,128)(2,1)}), bf16[4096,1024]{1,0:T(8,128)(2,1)}) %all-gather.5.cloned.1.call-update) | async-done | bytes 8388624 | tf_op jit(solution)/shard_map/all_gather | solution.py:127
  111.5 10.1 %fusion.31 = f32[512,4096]{1,0:T(8,128)} fusion(bf16[512,1024]{1,0:T(8,128)(2,1)S(1)} %bitcast.91, bf16[4096,1024]{1,0:T(8,128)(2,1)} %all-gather.5.cloned.1.call-done), kind=kOutput, calls=%fused_computation.57 | convolution fusion | flops 4294967296 | bytes 17825792 | tf_op jit(solution)/shard_map/dot_general | solution.py:131
  124.5 4.6 copy.57
  130.0 4.6 maximum_convert_fusion
  134.6 3.6 copy-done.2
  138.3 5.9 multiply_add_fusion
  144.2 58.5 %reduce-scatter.2.cloned.1.call-done = f32[512,1024]{1,0:T(8,128)} async-done(((f32[512,4096]{1,0:T(8,128)}), f32[512,1024]{1,0:T(8,128)}) %reduce-scatter.2.cloned.1.call-update) | async-done | bytes 2097168 | tf_op jit(solution)/shard_map/reduce_scatter | solution.py:137
  211.6 2.6 copy.97
  216.5 15.8 %reshape.121 = bf16[64,128,255,1,1]{2,1,0,3,4:T(8,128)(2,1)} reshape(bf16[64,32640]{1,0:T(8,128)(2,1)} %slice.126) | data formatting | bytes 8355840 | tf_op jit(solution)/shard_map/reshape | solution.py:37
  243.7 4.1 fusion.20
  250.3 3.9 reshape.116
  254.1 5.9 multiply_convert_fusion.1
  262.1 4.8 collective-permute-start.1
  267.3 2.6 copy.96
  272.2 16.0 %reshape.120 = bf16[64,128,255,1,1]{2,1,0,3,4:T(8,128)(2,1)} reshape(bf16[64,32640]{1,0:T(8,128)(2,1)} %slice.122) | data formatting | bytes 8355840 | tf_op jit(solution)/shard_map/reshape | solution.py:37
  294.2 3.3 squeeze.10
  297.5 3.9 fusion.26
  308.1 3.7 fusion.17
  312.9 2.7 reshape.109
  315.6 3.0 reshape.104
  318.7 6.2 %convolution_bitcast_fusion = f32[64,128,255]{2,1,0:T(8,128)} fusion(bf16[2,2,255,16,64]{2,3,1,0,4:T(8,128)(2,1)} %copy-done.5, bf16[2,2,128,16,64]{2,1,0,3,4:T(2,128)(2,1)S(1)} %copy-done.9), kind=kOutput, calls=%fused_computation.20 | convolution fusion | flops 267386880 | bytes 11493376 | tf_op jit(solution)/shard_map/sbtcg,sbjcg->gtj/dot_general | solution.py:53
  324.9 9.2 %reshape.118 = f32[64,32640]{1,0:T(8,128)} reshape(f32[64,128,255]{2,1,0:T(8,128)} %convolution_bitcast_fusion) | data formatting | bytes 16711680 | tf_op jit(solution)/shard_map/reshape | solution.py:60
  334.1 4.0 pad.16
  344.4 10.9 %fusion = (f32[3,1024]{1,0:T(4,128)S(1)}, f32[3,1024]{1,0:T(4,128)S(1)}, f32[3,1024]{1,0:T(4,128)S(1)}) fusion(f32[2,258,3,1024]{1,3,0,2:T(8,128)} %copy-done.2, bf16[2,256,1,1024]{1,3,0,2:T(8,128)(2,1)S(1)} %copy-done.4, bf16[2,256,1,1024]{1,3,0,2:T(8,128)(2,1)S(1)} %copy-done.3, bf16[2,256,1,1024]{1,3,0,2:T(8,128)(2,1)S(1)} %multiply_convert_fusion.2), kind=kLoop, calls=%fused_computation.3 | loop fusion | flops 14146560 | bytes 22056960 | tf_op jit(solution)/shard_map/reduce_sum | solution.py:93
  356.0 3.4 fusion.13
  364.2 3.3 collective-permute-done.3
  371.8 5.8 fusion.4
  377.6 4.6 copy.78
  382.2 145.3 %all-reduce.8.cloned.1.call-done = (f32[64,128]{1,0:T(8,128)}, f32[3,3,1024]{2,0,1:T(4,128)}) async-done(((f32[64,128]{1,0:T(8,128)}, f32[3,3,1024]{2,0,1:T(4,128)}), (f32[64,128]{1,0:T(8,128)}, f32[3,3,1024]{2,0,1:T(4,128)})) %all-reduce.8.cloned.1.call-update) | async-done | bytes 69648 | tf_op jit(solution)/shard_map/psum | solution.py:169
  530.4 46.8 %all-gather.3.cloned.1.call-done = bf16[2,256,4096]{1,2,0:T(8,128)(2,1)} async-done(((bf16[2,256,1024]{1,2,0:T(8,128)(2,1)}), bf16[2,256,4096]{1,2,0:T(8,128)(2,1)}) %all-gather.3.cloned.1.call-update) | async-done | bytes 4194320 | tf_op jit(solution)/shard_map/all_gather | solution.py:122
  577.3 6.5 %copy.63 = bf16[2,256,4096]{2,1,0:T(8,128)(2,1)} copy(bf16[2,256,4096]{1,2,0:T(8,128)(2,1)} %all-gather.3.cloned.1.call-done) | data formatting | bytes 8388608 | tf_op jit(solution)/shard_map/all_gather | solution.py:122
  583.8 10.2 %convolution_convert_fusion = bf16[512,1024]{1,0:T(8,128)(2,1)} fusion(bf16[512,4096]{1,0:T(8,128)(2,1)} %bitcast.102, bf16[4096,1024]{1,0:T(8,128)(2,1)} %all-gather.5.cloned.1.call-done), kind=kOutput, calls=%fused_computation.42 | convolution fusion | flops 4295491584 | bytes 13631488 | tf_op jit(solution)/shard_map/dot_general | solution.py:125
  (85 shorter events, 66.8 us)
Async XLA Ops:
  7.2 104.4 %copy-start = (bf16[2,256,1024]{2,1,0:T(8,128)(2,1)S(1)}, bf16[2,256,1024]{2,1,0:T(8,128)(2,1)}, u32[]{:S(2)}) copy-start(bf16[2,256,1024]{2,1,0:T(8,128)(2,1)} %param.9) | copy-start | bytes 3145732
  7.2 104.3 %all-gather.5.cloned.1.call-start = ((), (), s32[]{:S(2)}) async-start(), calls=%async_computation.2 | async-start | bytes 8650752 | tf_op jit(solution)/shard_map/all_gather | solution.py:127
  7.9 194.7 %reduce-scatter.2.cloned.1.call-start = ((), (), s32[]{:S(2)}) async-start(), calls=%async_computation.3 | async-start | bytes 10485760 | tf_op jit(solution)/shard_map/reduce_scatter | solution.py:137
  121.7 2.8 copy-start.11
  121.7 405.9 %all-reduce.8.cloned.1.call-start = ((), (), s32[]{:S(2)}) async-start(), calls=%async_computation.4 | async-start | bytes 163840 | tf_op jit(solution)/shard_map/psum | solution.py:169
  122.7 6.5 %collective-permute-start = (bf16[2,2,3,1024]{3,1,2,0:T(2,128)(2,1)S(1)}, bf16[2,2,3,1024]{3,1,2,0:T(2,128)(2,1)S(1)}, u32[]{:S(2)}, u32[]{:S(2)}) collective-permute-start(bf16[2,2,3,1024]{3,1,2,0:T(2,128)(2,1)S(1)} %slice.89), channel_id=1, source_target_pairs={{0,4},{4,8},{8,12},{12,16},{16,20},{20,24},{24,28},{28,32},{32,36}... | collective-permute-start | bytes 73736 | tf_op jit(solution)/shard_map/ppermute | solution.py:11
  134.6 3.7 copy-start.2
  206.4 4.8 copy-start.10
  208.9 2.4 copy-start.6
  209.8 22.5 %collective-permute-start.2 = (bf16[2,127,1024]{1,2,0:T(8,128)(2,1)}, bf16[2,127,1024]{1,2,0:T(8,128)(2,1)}, u32[]{:S(2)}, u32[]{:S(2)}) collective-permute-start(bf16[2,127,1024]{1,2,0:T(8,128)(2,1)} %slice.123), channel_id=1, source_target_pairs={{4,0},{8,4},{12,8},{16,12},{20,16},{24,20},{28,24},{32,28},{36,32}... | collective-permute-start | bytes 1560584 | tf_op jit(solution)/shard_map/ppermute | solution.py:11
  260.1 1.0 copy-start.7
  262.1 39.3 %collective-permute-start.1 = (bf16[2,127,1024]{1,2,0:T(8,128)(2,1)}, bf16[2,127,1024]{1,2,0:T(8,128)(2,1)}, u32[]{:S(2)}, u32[]{:S(2)}) collective-permute-start(bf16[2,127,1024]{1,2,0:T(8,128)(2,1)} %slice.119), channel_id=1, source_target_pairs={{0,4},{4,8},{8,12},{12,16},{16,20},{20,24},{24,28},{28,32},{32,36}... | collective-permute-start | bytes 1560584 | tf_op jit(solution)/shard_map/ppermute | solution.py:11
  297.5 3.9 copy-start.8
  306.7 1.3 copy-start.5
  315.6 3.0 copy-start.9
  341.2 3.2 copy-start.3
  341.2 3.2 copy-start.4
  355.9 221.4 %all-gather.3.cloned.1.call-start = ((), (), s32[]{:S(2)}) async-start(), calls=%async_computation.1 | async-start | bytes 5242880 | tf_op jit(solution)/shard_map/all_gather | solution.py:122
  362.9 4.6 collective-permute-start.3
  583.8 10.2 %copy-start.1 = (bf16[2,256,1024]{2,1,0:T(8,128)(2,1)S(1)}, bf16[2,256,1024]{2,1,0:T(8,128)(2,1)}, u32[]{:S(2)}) copy-start(bf16[2,256,1024]{2,1,0:T(8,128)(2,1)} %param.9) | copy-start | bytes 3145732
Sparse Core Ops, SparseCore 0:
  10.6 100.9 all-gather.4
  121.8 80.7 reduce-scatter.1
  356.0 171.5 all-reduce.7
  529.8 47.3 all-gather.2
where the time goes:
time: 607 us; the launch traced here: 601 us
  waiting for transfers between devices  358 us (59%)
  local copies, waits for them, and re-layouts  127 us (21%)
  other arithmetic  56.9 us (9%)
  matrix products  34.4 us (6%)
  between operations  14.3 us (2%)
  starting transfers between devices  9.42 us (2%)
    psum x1, waiting for transfers between devices, shards(): lax.psum((filter_part, short_part), ('dp', 'ctx'))  145 us
    all_gather x1, waiting for transfers between devices, shards(): lax.all_gather(out_w, 'ctx', axis=0, tiled=True)  104 us
    reduce_scatter x1, waiting for transfers between devices, shards(): lax.psum_scatter(input_part, 'grp', scatter_dimension=1, tiled=True)  58.5 us
    all_gather x1, waiting for transfers between devices, shards(): whole_gated = lax.all_gather(gated, 'grp', axis=2, tiled=True)  46.8 us
    reshape x2, local copies, waits for them, and re-layouts, banded(): tiled[:, :block_rows * (line_width - 1)]  31.8 us
    unnamed x34, local copies, waits for them, and re-layouts  25.5 us
  transfers between devices with their start and end apart: 8, of which 5 were waited for; matrix products, arithmetic and copies ran while one was open for 16% of the time, Pallas kernels for 0%

commit v1 on v0

--- a/solution.py
+++ b/solution.py
@@ -166,7 +166,7 @@
     short_part = short_sums(
         feature_grad.astype(jnp.float32), padded_input.astype(jnp.float32), short_taps
     )
-    filter_total, short_total = lax.psum((filter_part, short_part), ("dp", "ctx"))
+    filter_total, short_total = lax.psum(lax.psum((filter_part, short_part), "dp"), "ctx")
     seq_total = seq_local * lax.axis_size("dp")
     length_total = row_count * lax.axis_size("ctx")
     filter_grad = filter_total / math.sqrt(seq_total * length_total * group_size)

time: 607 us -> 610 us (level)
    psum x1 -> x2, waiting for transfers between devices: 145 us -> 142 us  [the longest x1 116 us: shards(): lax.psum(lax.psum((filter_part, short_part), 'dp'), 'ctx')]
    unnamed x34 -> x38, local copies, waits for them, and re-layouts: 25.5 us -> 25.6 us
  transfers between devices with their start and end apart: 8 -> 9, of which waited for: 5 -> 6; matrix products, arithmetic and copies ran while one was open for 16% -> 17% of each run, Pallas kernels for 0% -> 0%
where the time goes in v1:
time: 610 us; the launch traced here: 603 us
  waiting for transfers between devices  360 us (59%)
  local copies, waits for them, and re-layouts  128 us (21%)
  other arithmetic  57.5 us (9%)
  matrix products  34.4 us (6%)
  between operations  14.3 us (2%)
  starting transfers between devices  9.46 us (2%)
    psum x1, waiting for transfers between devices, shards(): lax.psum(lax.psum((filter_part, short_part), 'dp'), 'ctx')  116 us
    all_gather x1, waiting for transfers between devices, shards(): lax.all_gather(out_w, 'ctx', axis=0, tiled=True)  104 us
    reduce_scatter x1, waiting for transfers between devices, shards(): lax.psum_scatter(input_part, 'grp', scatter_dimension=1, tiled=True)  58.5 us
    all_gather x1, waiting for transfers between devices, shards(): whole_gated = lax.all_gather(gated, 'grp', axis=2, tiled=True)  51.6 us
    reshape x2, local copies, waits for them, and re-layouts, banded(): tiled[:, :block_rows * (line_width - 1)]  31.9 us
    psum x1, waiting for transfers between devices, shards(): lax.psum((filter_part, short_part), 'dp')  26.4 us
    unnamed x38, local copies, waits for them, and re-layouts  25.6 us
  transfers between devices with their start and end apart: 9, of which 6 were waited for; matrix products, arithmetic and copies ran while one was open for 17% of the time, Pallas kernels for 0%

profile of v1, /device:TPU:1, one launch (start us, length us, event | category | flops | bytes accessed | tf_op | source)
XLA Modules:
  0.0 603.0 jit_solution(9203216123000702300)
XLA Ops:
  8.0 103.6 %all-gather.5.cloned.1.call-done = bf16[4096,1024]{1,0:T(8,128)(2,1)} async-done(((bf16[128,1024]{1,0:T(8,128)(2,1)}), bf16[4096,1024]{1,0:T(8,128)(2,1)}) %all-gather.5.cloned.1.call-update) | async-done | bytes 8388624 | tf_op jit(solution)/shard_map/all_gather | solution.py:127
  111.5 10.2 %fusion.31 = f32[512,4096]{1,0:T(8,128)} fusion(bf16[512,1024]{1,0:T(8,128)(2,1)S(1)} %bitcast.91, bf16[4096,1024]{1,0:T(8,128)(2,1)} %all-gather.5.cloned.1.call-done), kind=kOutput, calls=%fused_computation.57 | convolution fusion | flops 4294967296 | bytes 17825792 | tf_op jit(solution)/shard_map/dot_general | solution.py:131
  124.5 4.6 copy.57
  130.1 4.6 maximum_convert_fusion
  134.6 3.7 copy-done.2
  138.3 5.9 multiply_add_fusion
  144.2 58.5 %reduce-scatter.2.cloned.1.call-done = f32[512,1024]{1,0:T(8,128)} async-done(((f32[512,4096]{1,0:T(8,128)}), f32[512,1024]{1,0:T(8,128)}) %reduce-scatter.2.cloned.1.call-update) | async-done | bytes 2097168 | tf_op jit(solution)/shard_map/reduce_scatter | solution.py:137
  211.6 2.6 copy.97
  216.5 15.8 %reshape.121 = bf16[64,128,255,1,1]{2,1,0,3,4:T(8,128)(2,1)} reshape(bf16[64,32640]{1,0:T(8,128)(2,1)} %slice.126) | data formatting | bytes 8355840 | tf_op jit(solution)/shard_map/reshape | solution.py:37
  243.7 4.1 fusion.20
  250.3 3.9 reshape.116
  254.2 5.9 multiply_convert_fusion.1
  262.1 4.8 collective-permute-start.1
  272.2 16.0 %reshape.120 = bf16[64,128,255,1,1]{2,1,0,3,4:T(8,128)(2,1)} reshape(bf16[64,32640]{1,0:T(8,128)(2,1)} %slice.122) | data formatting | bytes 8355840 | tf_op jit(solution)/shard_map/reshape | solution.py:37
  294.2 3.3 squeeze.10
  297.5 3.9 fusion.26
  308.0 3.7 fusion.17
  312.9 2.7 reshape.109
  315.6 6.2 %convolution_bitcast_fusion = f32[64,128,255]{2,1,0:T(8,128)} fusion(bf16[2,2,255,16,64]{2,3,1,0,4:T(8,128)(2,1)} %copy-done.7, bf16[2,2,128,16,64]{2,1,0,3,4:T(2,128)(2,1)S(1)} %copy-done.11), kind=kOutput, calls=%fused_computation.20 | convolution fusion | flops 267386880 | bytes 11493376 | tf_op jit(solution)/shard_map/sbtcg,sbjcg->gtj/dot_general | solution.py:53
  321.8 9.6 %reshape.118 = f32[64,32640]{1,0:T(8,128)} reshape(f32[64,128,255]{2,1,0:T(8,128)} %convolution_bitcast_fusion) | data formatting | bytes 16711680 | tf_op jit(solution)/shard_map/reshape | solution.py:60
  331.5 4.0 pad.16
  342.0 11.2 %fusion = (f32[3,1024]{1,0:T(4,128)S(1)}, f32[3,1024]{1,0:T(4,128)S(1)}, f32[3,1024]{1,0:T(4,128)S(1)}) fusion(f32[2,258,3,1024]{1,3,0,2:T(8,128)} %copy-done.2, bf16[2,256,1,1024]{1,3,0,2:T(8,128)(2,1)S(1)} %copy-done.5, bf16[2,256,1,1024]{1,3,0,2:T(8,128)(2,1)S(1)} %copy-done.3, bf16[2,256,1,1024]{1,3,0,2:T(8,128)(2,1)S(1)} %multiply_convert_fusion.2), kind=kLoop, calls=%fused_computation.3 | loop fusion | flops 14146560 | bytes 22056960 | tf_op jit(solution)/shard_map/reduce_sum | solution.py:93
  353.9 2.7 reshape.104
  356.6 26.4 %all-reduce.12.cloned.1.call-done = (f32[64,128]{1,0:T(8,128)}, f32[3,3,1024]{2,0,1:T(4,128)}) async-done(((f32[64,128]{1,0:T(8,128)}, f32[3,3,1024]{2,0,1:T(4,128)}), (f32[64,128]{1,0:T(8,128)}, f32[3,3,1024]{2,0,1:T(4,128)})) %all-reduce.12.cloned.1.call-update) | async-done | bytes 69648 | tf_op jit(solution)/shard_map/psum | solution.py:169
  383.1 3.6 fusion.13
  391.5 3.3 collective-permute-done.3
  399.2 5.8 fusion.4
  405.0 4.6 copy.78
  409.6 115.5 %all-reduce.10.cloned.1.call-done = (f32[64,128]{1,0:T(8,128)}, f32[3,3,1024]{2,0,1:T(4,128)}) async-done(((f32[64,128]{1,0:T(8,128)}, f32[3,3,1024]{2,0,1:T(4,128)}), (f32[64,128]{1,0:T(8,128)}, f32[3,3,1024]{2,0,1:T(4,128)})) %all-reduce.10.cloned.1.call-update) | async-done | bytes 69648 | tf_op jit(solution)/shard_map/psum | solution.py:169
  528.0 51.6 %all-gather.3.cloned.1.call-done = bf16[2,256,4096]{1,2,0:T(8,128)(2,1)} async-done(((bf16[2,256,1024]{1,2,0:T(8,128)(2,1)}), bf16[2,256,4096]{1,2,0:T(8,128)(2,1)}) %all-gather.3.cloned.1.call-update) | async-done | bytes 4194320 | tf_op jit(solution)/shard_map/all_gather | solution.py:122
  579.6 6.5 %copy.63 = bf16[2,256,4096]{2,1,0:T(8,128)(2,1)} copy(bf16[2,256,4096]{1,2,0:T(8,128)(2,1)} %all-gather.3.cloned.1.call-done) | data formatting | bytes 8388608 | tf_op jit(solution)/shard_map/all_gather | solution.py:122
  586.1 10.2 %convolution_convert_fusion = bf16[512,1024]{1,0:T(8,128)(2,1)} fusion(bf16[512,4096]{1,0:T(8,128)(2,1)} %bitcast.102, bf16[4096,1024]{1,0:T(8,128)(2,1)} %all-gather.5.cloned.1.call-done), kind=kOutput, calls=%fused_computation.42 | convolution fusion | flops 4295491584 | bytes 13631488 | tf_op jit(solution)/shard_map/dot_general | solution.py:125
  (92 shorter events, 69.7 us)
Async XLA Ops:
  7.2 104.4 %copy-start = (bf16[2,256,1024]{2,1,0:T(8,128)(2,1)S(1)}, bf16[2,256,1024]{2,1,0:T(8,128)(2,1)}, u32[]{:S(2)}) copy-start(bf16[2,256,1024]{2,1,0:T(8,128)(2,1)} %param.9) | copy-start | bytes 3145732
  7.2 104.3 %all-gather.5.cloned.1.call-start = ((), (), s32[]{:S(2)}) async-start(), calls=%async_computation.2 | async-start | bytes 8650752 | tf_op jit(solution)/shard_map/all_gather | solution.py:127
  7.9 194.7 %reduce-scatter.2.cloned.1.call-start = ((), (), s32[]{:S(2)}) async-start(), calls=%async_computation.3 | async-start | bytes 10485760 | tf_op jit(solution)/shard_map/reduce_scatter | solution.py:137
  121.7 2.8 copy-start.13
  121.7 261.3 %all-reduce.12.cloned.1.call-start = ((), (), s32[]{:S(2)}) async-start(), calls=%async_computation.5 | async-start | bytes 163840 | tf_op jit(solution)/shard_map/psum | solution.py:169
  122.7 6.5 %collective-permute-start = (bf16[2,2,3,1024]{3,1,2,0:T(2,128)(2,1)S(1)}, bf16[2,2,3,1024]{3,1,2,0:T(2,128)(2,1)S(1)}, u32[]{:S(2)}, u32[]{:S(2)}) collective-permute-start(bf16[2,2,3,1024]{3,1,2,0:T(2,128)(2,1)S(1)} %slice.89), channel_id=1, source_target_pairs={{0,4},{4,8},{8,12},{12,16},{16,20},{20,24},{24,28},{28,32},{32,36}... | collective-permute-start | bytes 73736 | tf_op jit(solution)/shard_map/ppermute | solution.py:11
  134.6 3.7 copy-start.2
  206.5 4.8 copy-start.12
  208.9 2.4 copy-start.8
  209.8 22.5 %collective-permute-start.2 = (bf16[2,127,1024]{1,2,0:T(8,128)(2,1)}, bf16[2,127,1024]{1,2,0:T(8,128)(2,1)}, u32[]{:S(2)}, u32[]{:S(2)}) collective-permute-start(bf16[2,127,1024]{1,2,0:T(8,128)(2,1)} %slice.123), channel_id=1, source_target_pairs={{4,0},{8,4},{12,8},{16,12},{20,16},{24,20},{28,24},{32,28},{36,32}... | collective-permute-start | bytes 1560584 | tf_op jit(solution)/shard_map/ppermute | solution.py:11
  260.1 1.0 copy-start.9
  262.1 39.3 %collective-permute-start.1 = (bf16[2,127,1024]{1,2,0:T(8,128)(2,1)}, bf16[2,127,1024]{1,2,0:T(8,128)(2,1)}, u32[]{:S(2)}, u32[]{:S(2)}) collective-permute-start(bf16[2,127,1024]{1,2,0:T(8,128)(2,1)} %slice.119), channel_id=1, source_target_pairs={{0,4},{4,8},{8,12},{12,16},{16,20},{20,24},{24,28},{28,32},{32,36}... | collective-permute-start | bytes 1560584 | tf_op jit(solution)/shard_map/ppermute | solution.py:11
  297.5 3.9 copy-start.10
  306.8 1.3 copy-start.7
  312.9 2.7 copy-start.11
  339.2 2.6 copy-start.3
  339.2 2.8 copy-start.5
  353.9 171.3 %all-reduce.10.cloned.1.call-start = ((), (), s32[]{:S(2)}) async-start(), calls=%async_computation.4 | async-start | bytes 163840 | tf_op jit(solution)/shard_map/psum | solution.py:169
  383.0 3.7 copy-start.4
  383.0 3.7 copy-start.6
  383.0 196.6 %all-gather.3.cloned.1.call-start = ((), (), s32[]{:S(2)}) async-start(), calls=%async_computation.1 | async-start | bytes 5242880 | tf_op jit(solution)/shard_map/all_gather | solution.py:122
  390.2 4.6 collective-permute-start.3
  586.1 10.2 %copy-start.1 = (bf16[2,256,1024]{2,1,0:T(8,128)(2,1)S(1)}, bf16[2,256,1024]{2,1,0:T(8,128)(2,1)}, u32[]{:S(2)}) copy-start(bf16[2,256,1024]{2,1,0:T(8,128)(2,1)} %param.9) | copy-start | bytes 3145732
Sparse Core Ops, SparseCore 0:
  10.6 100.9 all-gather.4
  121.8 80.7 reduce-scatter.1
  354.0 28.9 all-reduce.11
  386.3 138.7 all-reduce.9
  526.8 52.7 all-gather.2
